TPU v7x, 32 devices: a whole 2x2x4 slice. The times are simulated.
32 devices in a mesh: tiles: 8 (over z, x), chan: 4 (over y, core).
Axes of the slice: x: 2, y: 2, z: 4, core: 2. Of those that a mesh axis runs over, the one named last changes fastest.
Arguments:
- features: bfloat16 [512, 64, 256], P('tiles'), may hold values from -6 to 6
- weights: bfloat16 [27, 256, 256], P(None, None, 'chan')
- gain: bfloat16 [256], P('chan'), may hold values from 0.099609375 to 1.8984375
- rulebook: int32 [6144, 4], P('tiles'), may hold values from 0 to 191, as said below
- recv_list: int32 [8, 128], P('tiles'), may hold values from 0 to 63, as said below
- coarse_send: int32 [8, 8], P('tiles'), may hold values from 0 to 7, as said below
- coarse_place: int32 [8, 8], P('tiles'), may hold values from 0 to 7, as said below
Outputs:
- skip_features: bfloat16 [512, 64, 256], P('tiles', None, 'chan')
- coarse_features: bfloat16 [64, 64, 256], P('tiles', None, 'chan')
Inputs may be any that keep to these rules, and one draw needn't show every extreme that they name: `rulebook`: Columns: input tile 0 to 63 of the device; kernel offset 0 to 26, or 27 for an empty row; direction 0 to 26, the input tile's place relative to the output tile, along each dimension 0 or equal to the kernel offset's nonzero component; target below 64 a tile of the device, else slot s = target - 64 for device d + dist(s // 16), which always exists. Empty rows have 0 in the other columns and direction 13. Each device has 192 or more live rows, some device none empty; every slot toward an existing device is named by a live row, and every tile has a row with offset 13, direction 13 and itself as input and target. `recv_list`: each tile of a device is named exactly twice in its row. `coarse_send`: strided owner map: coarse tile k of device s, global number p = s * 8 + k, goes to an owner that depends only on p % 8 (a permutation of the devices), in lane k // 8; slots of one row are distinct. `coarse_place`: the slot s + j of owner e holds the place of the coarse tile it receives; 8 marks a slot that carries nothing. Every coarse tile of the owner is written by exactly one slot.
All inputs are finite; a program needn't handle non-finite values.
Results may differ from a plain program's by a relative error of at most 0.0045.
Values may be sent and summed in bfloat16 or wider, within the bound.
No kernel may reach another device: no remote copies, remote signals or barrier semaphores. Data moves between devices by JAX's collectives and lax.ppermute only.
A program may use at most 128 MiB of HBM per device.

v0:
```python
import jax
import jax.numpy as jnp
from jax import lax
from jax.sharding import PartitionSpec as P

epsilon = 1e-05


def from_behind(block, axis, distance):
    devices = range(lax.axis_size(axis))
    route = [(i - distance, i) for i in devices if i - distance in devices]
    return lax.ppermute(block, axis, route)


def offsets(code):
    return jnp.stack([code // 9 - 1, code // 3 % 3 - 1, code % 3 - 1], axis=-1)


def shift_table(kernel, heading):
    voxel = jnp.arange(64, dtype=jnp.int32)
    corner = jnp.stack([voxel // 16, voxel // 4 % 4, voxel % 4], axis=-1)
    source = (
        corner[None, :, :]
        + offsets(jnp.minimum(kernel, 26))[:, None, :]
        - 4 * offsets(heading)[:, None, :]
    )
    inside = jnp.all((source >= 0) & (source < 4), axis=-1) & (kernel < 27)[:, None]
    source = jnp.clip(source, 0, 3)
    where_from = source[..., 0] * 16 + source[..., 1] * 4 + source[..., 2]
    return (where_from, inside)


def pool_blocks(values):
    dims_in = values.shape
    blocked = values.astype(jnp.float32).reshape(dims_in[:-2] + (2, 2, 2, 2, 2, 2, dims_in[-1]))
    return (
        jnp.mean(blocked, axis=(-6, -4, -2))
        .reshape(dims_in[:-2] + (8, dims_in[-1]))
        .astype(jnp.bfloat16)
    )


def assemble(placed):
    number = placed.shape[0]
    blocked = placed.reshape(number, 2, 2, 2, 2, 2, 2, placed.shape[-1])
    return blocked.transpose(0, 1, 4, 2, 5, 3, 6, 7).reshape(number, 64, placed.shape[-1])


def body(features, weights, gain, rulebook, recv_list, coarse_send, coarse_place):
    tile_count = features.shape[0]
    channels = features.shape[2]
    quarter = weights.shape[2]
    rule_rows = rulebook.shape[0]
    block_rows = min(128, rule_rows)
    slot_width = tile_count // 4
    chan_pos = lax.axis_index("chan")
    own_part = lax.dynamic_slice_in_dim(features, chan_pos * quarter, quarter, 2)
    grouped = rulebook.reshape(rule_rows // block_rows, block_rows, 4)
    voxel = jnp.arange(64, dtype=jnp.int32)
    tile_ids = jnp.arange(tile_count, dtype=jnp.int32)
    target_ids = jnp.arange(3 * tile_count, dtype=jnp.int32)
    flat_features = features.reshape(tile_count, 64 * channels)

    def step_rules(totals, group):
        where_from, inside = shift_table(group[:, 1], group[:, 2])
        picker = ((where_from[:, :, None] == voxel[None, None, :]) & inside[:, :, None]).astype(
            jnp.bfloat16
        )
        source_hot = (group[:, 0][:, None] == tile_ids[None, :]).astype(jnp.bfloat16)
        fetched = jnp.dot(source_hot, flat_features, preferred_element_type=jnp.float32).astype(
            jnp.bfloat16
        )
        fetched = fetched.reshape(group.shape[0], 64, channels)
        chosen = jnp.einsum(
            "bvu,buc->bvc", picker, fetched, preferred_element_type=jnp.float32
        ).astype(jnp.bfloat16)
        kernels = weights[jnp.minimum(group[:, 1], 26)]
        partial_out = jnp.einsum(
            "bvc,bcq->bvq", chosen, kernels, preferred_element_type=jnp.float32
        )
        target_hot = (target_ids[:, None] == group[:, 3][None, :]).astype(jnp.float32)
        added = jnp.dot(
            target_hot,
            partial_out.reshape(group.shape[0], 64 * quarter),
            precision=lax.Precision.HIGHEST,
            preferred_element_type=jnp.float32,
        )
        return (totals + added.reshape(3 * tile_count, 64, quarter), None)

    start = jnp.zeros((3 * tile_count, 64, quarter), jnp.float32)
    totals, unused = lax.scan(step_rules, start, grouped)
    outgoing = totals[tile_count:].astype(jnp.bfloat16).reshape(8, slot_width, 64, quarter)
    arrivals = []
    for group in range(8):
        distance = group + 1 if group < 4 else 3 - group
        arrivals.append(from_behind(outgoing[group], "tiles", distance))
    incoming = jnp.stack(arrivals, axis=0).reshape(2 * tile_count, 64 * quarter)
    receive_hot = (tile_ids[:, None] == recv_list[0][None, :]).astype(jnp.bfloat16)
    gathered_in = jnp.dot(receive_hot, incoming, preferred_element_type=jnp.float32).reshape(
        tile_count, 64, quarter
    )
    convolved = totals[:tile_count] + gathered_in
    squares = lax.psum(jnp.sum(convolved * convolved, axis=-1), "chan")
    mean_square = squares[:, :, None] / channels
    hidden = jax.nn.silu(gain.astype(jnp.float32) * convolved * lax.rsqrt(mean_square + epsilon))
    skip_features = (own_part.astype(jnp.float32) + hidden).astype(jnp.bfloat16)
    pooled = pool_blocks(skip_features)
    parents = assemble(pooled.reshape(tile_count // 8, 8, 8, quarter))
    slot_count = coarse_place.shape[1]
    parent_count = tile_count // 8
    slot_ids = jnp.arange(slot_count, dtype=jnp.int32)
    parent_ids = jnp.arange(parent_count, dtype=jnp.int32)
    send_hot = (slot_ids[:, None] == coarse_send[0][None, :]).astype(jnp.bfloat16)
    outbound = jnp.dot(
        send_hot, parents.reshape(parent_count, 64 * quarter), preferred_element_type=jnp.float32
    ).astype(jnp.bfloat16)
    outbound = outbound.reshape(slot_count, 64, quarter)
    landed = lax.all_to_all(outbound, "tiles", split_axis=0, concat_axis=0, tiled=True)
    place_hot = (parent_ids[:, None] == coarse_place[0][None, :]).astype(jnp.bfloat16)
    coarse_features = jnp.dot(
        place_hot, landed.reshape(slot_count, 64 * quarter), preferred_element_type=jnp.float32
    ).astype(jnp.bfloat16)
    coarse_features = coarse_features.reshape(parent_count, 64, quarter)
    return (skip_features, coarse_features)


def solution(mesh):
    in_specs = (
        P("tiles", None, None),
        P(None, None, "chan"),
        P("chan"),
        P("tiles", None),
        P("tiles", None),
        P("tiles", None),
        P("tiles", None),
    )
    out_specs = (P("tiles", None, "chan"), P("tiles", None, "chan"))
    return jax.shard_map(body, mesh=mesh, in_specs=in_specs, out_specs=out_specs, check_vma=False)
```

profile of v0, /device:TPU:0, one launch (start us, length us, event | category | flops | bytes accessed | tf_op | source)
XLA Modules:
  0.0 264.5 jit_solution(9480351480479693915)
XLA Ops:
  0.7 4.3 %copy.38 = bf16[8,8,64,256]{3,1,2,0:T(8,128)(2,1)} copy(bf16[8,8,64,256]{3,2,1,0:T(8,128)(2,1)} %bitcast.91) | data formatting | bytes 4194304
  4.9 160.6 %while.16 = (s32[]{:T(128)}, f32[192,64,64]{0,2,1:T(8,128)}, s32[6,128,4]{1,2,0:T(4,128)}, bf16[64,16384]{1,0:T(8,128)(2,1)}, bf16[27,256,64]{1,2,0:T(8,128)(2,1)S(1)}, /*index=5*/s32[]{:T(128)}, s32[]{:T(128)}) while((s32[]{:T(128)}, f32[192,64,64]{0,2,1:T(8,128)}, s32[6,128,4]{1,2,0:T(4,128)}, ...), condition=%wide.region_2.3_spmd.clone.clone, body=%wide.region_0.2_spmd.clone.clone.sunk | while | flops 2020381184 | bytes 46548056 | solution.py:91
  15.1 7.2 %fusion.70 = f32[128,64,64]{2,1,0:T(8,128)} fusion(bf16[128,256,64]{1,2,0:T(8,128)(2,1)} %gather_fusion, bf16[128,64,256]{2,1,0:T(8,128)(2,1)} %bitcast.88, s32[128,64]{1,0:T(8,128)S(1)} %copy.44, pred[128,64]{1,0:T(8,128)(4,1)S(1)} %copy.45), kind=kOutput, calls=%fused_computation.6.clone.1 | convolution fusion | flops 540016640 | bytes 10526720 | tf_op jit(solution)/shard_map/while/body/eval_jaxpr/bvc,bcq->bvq/dot_general | solution.py:78
  22.3 3.8 %copy.46 = f32[128,64,64]{0,2,1:T(8,128)S(1)} copy(f32[128,64,64]{2,1,0:T(8,128)} %fusion.70) | data formatting | bytes 4194304 | tf_op jit(solution)/shard_map/while/body/eval_jaxpr/bvc,bcq->bvq/dot_general | solution.py:78
  26.1 3.8 %select_add_fusion.2 = f32[192,64,64]{0,2,1:T(8,128)} fusion(f32[192,64,64]{0,2,1:T(8,128)} %get-tuple-element.311, f32[128,64,64]{0,2,1:T(8,128)S(1)} %copy.46, pred[]{:T(512)S(6)} %compare.18, s32[128]{0:T(128)S(1)} %get-tuple-element.302), kind=kOutput, calls=%fused_computation.5.clone.1 | convolution fusion | flops 1209556992 | bytes 8389121 | tf_op jit(solution)/shard_map/while/body/eval_jaxpr/dot_general | solution.py:82
  40.0 7.2 %fusion.70 = f32[128,64,64]{2,1,0:T(8,128)} fusion(bf16[128,256,64]{1,2,0:T(8,128)(2,1)} %gather_fusion, bf16[128,64,256]{2,1,0:T(8,128)(2,1)} %bitcast.88, s32[128,64]{1,0:T(8,128)S(1)} %copy.44, pred[128,64]{1,0:T(8,128)(4,1)S(1)} %copy.45), kind=kOutput, calls=%fused_computation.6.clone.1 | convolution fusion | flops 540016640 | bytes 10526720 | tf_op jit(solution)/shard_map/while/body/eval_jaxpr/bvc,bcq->bvq/dot_general | solution.py:78
  47.2 3.8 %copy.46 = f32[128,64,64]{0,2,1:T(8,128)S(1)} copy(f32[128,64,64]{2,1,0:T(8,128)} %fusion.70) | data formatting | bytes 4194304 | tf_op jit(solution)/shard_map/while/body/eval_jaxpr/bvc,bcq->bvq/dot_general | solution.py:78
  51.0 6.0 %select_add_fusion.2 = f32[192,64,64]{0,2,1:T(8,128)} fusion(f32[192,64,64]{0,2,1:T(8,128)} %get-tuple-element.311, f32[128,64,64]{0,2,1:T(8,128)S(1)} %copy.46, pred[]{:T(512)S(6)} %compare.18, s32[128]{0:T(128)S(1)} %get-tuple-element.302), kind=kOutput, calls=%fused_computation.5.clone.1 | convolution fusion | flops 1209556992 | bytes 8389121 | tf_op jit(solution)/shard_map/while/body/eval_jaxpr/dot_general | solution.py:82
  67.1 7.2 %fusion.70 = f32[128,64,64]{2,1,0:T(8,128)} fusion(bf16[128,256,64]{1,2,0:T(8,128)(2,1)} %gather_fusion, bf16[128,64,256]{2,1,0:T(8,128)(2,1)} %bitcast.88, s32[128,64]{1,0:T(8,128)S(1)} %copy.44, pred[128,64]{1,0:T(8,128)(4,1)S(1)} %copy.45), kind=kOutput, calls=%fused_computation.6.clone.1 | convolution fusion | flops 540016640 | bytes 10526720 | tf_op jit(solution)/shard_map/while/body/eval_jaxpr/bvc,bcq->bvq/dot_general | solution.py:78
  74.4 3.8 %copy.46 = f32[128,64,64]{0,2,1:T(8,128)S(1)} copy(f32[128,64,64]{2,1,0:T(8,128)} %fusion.70) | data formatting | bytes 4194304 | tf_op jit(solution)/shard_map/while/body/eval_jaxpr/bvc,bcq->bvq/dot_general | solution.py:78
  78.2 6.0 %select_add_fusion.2 = f32[192,64,64]{0,2,1:T(8,128)} fusion(f32[192,64,64]{0,2,1:T(8,128)} %get-tuple-element.311, f32[128,64,64]{0,2,1:T(8,128)S(1)} %copy.46, pred[]{:T(512)S(6)} %compare.18, s32[128]{0:T(128)S(1)} %get-tuple-element.302), kind=kOutput, calls=%fused_computation.5.clone.1 | convolution fusion | flops 1209556992 | bytes 8389121 | tf_op jit(solution)/shard_map/while/body/eval_jaxpr/dot_general | solution.py:82
  88.3 3.2 %copy.43 = bf16[16,8,64,256]{3,2,1,0:T(8,128)(2,1)} copy(bf16[16,8,64,256]{3,1,2,0:T(8,128)(2,1)S(1)} %bitcast.89) | data formatting | bytes 8388608 | tf_op jit(solution)/shard_map/while
  94.3 7.2 %fusion.70 = f32[128,64,64]{2,1,0:T(8,128)} fusion(bf16[128,256,64]{1,2,0:T(8,128)(2,1)} %gather_fusion, bf16[128,64,256]{2,1,0:T(8,128)(2,1)} %bitcast.88, s32[128,64]{1,0:T(8,128)S(1)} %copy.44, pred[128,64]{1,0:T(8,128)(4,1)S(1)} %copy.45), kind=kOutput, calls=%fused_computation.6.clone.1 | convolution fusion | flops 540016640 | bytes 10526720 | tf_op jit(solution)/shard_map/while/body/eval_jaxpr/bvc,bcq->bvq/dot_general | solution.py:78
  101.5 3.8 %copy.46 = f32[128,64,64]{0,2,1:T(8,128)S(1)} copy(f32[128,64,64]{2,1,0:T(8,128)} %fusion.70) | data formatting | bytes 4194304 | tf_op jit(solution)/shard_map/while/body/eval_jaxpr/bvc,bcq->bvq/dot_general | solution.py:78
  105.3 6.0 %select_add_fusion.2 = f32[192,64,64]{0,2,1:T(8,128)} fusion(f32[192,64,64]{0,2,1:T(8,128)} %get-tuple-element.311, f32[128,64,64]{0,2,1:T(8,128)S(1)} %copy.46, pred[]{:T(512)S(6)} %compare.18, s32[128]{0:T(128)S(1)} %get-tuple-element.302), kind=kOutput, calls=%fused_computation.5.clone.1 | convolution fusion | flops 1209556992 | bytes 8389121 | tf_op jit(solution)/shard_map/while/body/eval_jaxpr/dot_general | solution.py:82
  121.4 7.2 %fusion.70 = f32[128,64,64]{2,1,0:T(8,128)} fusion(bf16[128,256,64]{1,2,0:T(8,128)(2,1)} %gather_fusion, bf16[128,64,256]{2,1,0:T(8,128)(2,1)} %bitcast.88, s32[128,64]{1,0:T(8,128)S(1)} %copy.44, pred[128,64]{1,0:T(8,128)(4,1)S(1)} %copy.45), kind=kOutput, calls=%fused_computation.6.clone.1 | convolution fusion | flops 540016640 | bytes 10526720 | tf_op jit(solution)/shard_map/while/body/eval_jaxpr/bvc,bcq->bvq/dot_general | solution.py:78
  128.6 3.8 %copy.46 = f32[128,64,64]{0,2,1:T(8,128)S(1)} copy(f32[128,64,64]{2,1,0:T(8,128)} %fusion.70) | data formatting | bytes 4194304 | tf_op jit(solution)/shard_map/while/body/eval_jaxpr/bvc,bcq->bvq/dot_general | solution.py:78
  132.4 6.0 %select_add_fusion.2 = f32[192,64,64]{0,2,1:T(8,128)} fusion(f32[192,64,64]{0,2,1:T(8,128)} %get-tuple-element.311, f32[128,64,64]{0,2,1:T(8,128)S(1)} %copy.46, pred[]{:T(512)S(6)} %compare.18, s32[128]{0:T(128)S(1)} %get-tuple-element.302), kind=kOutput, calls=%fused_computation.5.clone.1 | convolution fusion | flops 1209556992 | bytes 8389121 | tf_op jit(solution)/shard_map/while/body/eval_jaxpr/dot_general | solution.py:82
  148.5 7.2 %fusion.70 = f32[128,64,64]{2,1,0:T(8,128)} fusion(bf16[128,256,64]{1,2,0:T(8,128)(2,1)} %gather_fusion, bf16[128,64,256]{2,1,0:T(8,128)(2,1)} %bitcast.88, s32[128,64]{1,0:T(8,128)S(1)} %copy.44, pred[128,64]{1,0:T(8,128)(4,1)S(1)} %copy.45), kind=kOutput, calls=%fused_computation.6.clone.1 | convolution fusion | flops 540016640 | bytes 10526720 | tf_op jit(solution)/shard_map/while/body/eval_jaxpr/bvc,bcq->bvq/dot_general | solution.py:78
  155.7 3.8 %copy.46 = f32[128,64,64]{0,2,1:T(8,128)S(1)} copy(f32[128,64,64]{2,1,0:T(8,128)} %fusion.70) | data formatting | bytes 4194304 | tf_op jit(solution)/shard_map/while/body/eval_jaxpr/bvc,bcq->bvq/dot_general | solution.py:78
  159.5 6.0 %select_add_fusion.2 = f32[192,64,64]{0,2,1:T(8,128)} fusion(f32[192,64,64]{0,2,1:T(8,128)} %get-tuple-element.311, f32[128,64,64]{0,2,1:T(8,128)S(1)} %copy.46, pred[]{:T(512)S(6)} %compare.18, s32[128]{0:T(128)S(1)} %get-tuple-element.302), kind=kOutput, calls=%fused_computation.5.clone.1 | convolution fusion | flops 1209556992 | bytes 8389121 | tf_op jit(solution)/shard_map/while/body/eval_jaxpr/dot_general | solution.py:82
  165.5 6.2 %copy.31 = bf16[192,64,64]{2,1,0:T(8,128)(2,1)} copy(f32[192,64,64]{0,2,1:T(8,128)} %get-tuple-element.164) | data formatting | bytes 4718592 | tf_op jit(solution)/shard_map/while | solution.py:91
  174.3 5.5 %collective-permute-start = (bf16[16,64,64]{2,1,0:T(8,128)(2,1)}, bf16[16,64,64]{2,1,0:T(8,128)(2,1)}, u32[]{:S(2)}, u32[]{:S(2)}) collective-permute-start(bf16[16,64,64]{2,1,0:T(8,128)(2,1)} %get-tuple-element.243), channel_id=1, source_target_pairs={{0,4},{4,8},{8,12},{12,16},{16,20},{20,24},{24,28},{1,5},{5,9},{9,... | collective-permute-start | bytes 393224 | tf_op jit(solution)/shard_map/ppermute | solution.py:12
  179.8 3.5 %collective-permute-start.1 = (bf16[16,64,64]{2,1,0:T(8,128)(2,1)}, bf16[16,64,64]{2,1,0:T(8,128)(2,1)}, u32[]{:S(2)}, u32[]{:S(2)}) collective-permute-start(bf16[16,64,64]{2,1,0:T(8,128)(2,1)} %get-tuple-element.242), channel_id=1, source_target_pairs={{0,8},{4,12},{8,16},{12,20},{16,24},{20,28},{1,9},{5,13},{9,17},{1... | collective-permute-start | bytes 393224 | tf_op jit(solution)/shard_map/ppermute | solution.py:12
  183.4 4.5 %collective-permute-start.2 = (bf16[16,64,64]{2,1,0:T(8,128)(2,1)}, bf16[16,64,64]{2,1,0:T(8,128)(2,1)}, u32[]{:S(2)}, u32[]{:S(2)}) collective-permute-start(bf16[16,64,64]{2,1,0:T(8,128)(2,1)} %get-tuple-element.241), channel_id=1, source_target_pairs={{0,12},{4,16},{8,20},{12,24},{16,28},{1,13},{5,17},{9,21},{13,25},... | collective-permute-start | bytes 393224 | tf_op jit(solution)/shard_map/ppermute | solution.py:12
  207.9 6.2 %collective-permute-done.6 = bf16[16,64,64]{2,1,0:T(8,128)(2,1)S(1)} collective-permute-done((bf16[16,64,64]{2,1,0:T(8,128)(2,1)S(1)}, bf16[16,64,64]{2,1,0:T(8,128)(2,1)S(1)}, u32[]{:S(2)}, u32[]{:S(2)}) %collective-permute-start.6) | collective-permute-done | bytes 131104 | tf_op jit(solution)/shard_map/ppermute | solution.py:12
  214.8 14.5 %collective-permute-done.7 = bf16[16,64,64]{2,1,0:T(8,128)(2,1)S(1)} collective-permute-done((bf16[16,64,64]{2,1,0:T(8,128)(2,1)S(1)}, bf16[16,64,64]{2,1,0:T(8,128)(2,1)S(1)}, u32[]{:S(2)}, u32[]{:S(2)}) %collective-permute-start.7) | collective-permute-done | bytes 131104 | tf_op jit(solution)/shard_map/ppermute | solution.py:12
  230.1 3.3 %reshape.246 = bf16[128,4096]{1,0:T(8,128)(2,1)S(1)} reshape(bf16[8,16,64,64]{3,2,1,0:T(8,128)(2,1)} %bitcast_dynamic-update-slice_fusion) | data formatting | bytes 2097152 | tf_op jit(solution)/shard_map/reshape | solution.py:97
  234.7 3.7 %multiply_reduce_fusion = (f32[64,64]{0,1:T(8,128)S(1)}, f32[64,64,64]{0,2,1:T(8,128)}) fusion(bf16[64,64,128]{2,1,0:T(8,128)(2,1)} %bitcast.93, s32[128]{0:T(128)S(1)} %bitcast.98, f32[192,64,64]{0,2,1:T(8,128)} %get-tuple-element.164), kind=kOutput, calls=%fused_computation.71 | convolution fusion | flops 67899392 | bytes 3162624 | tf_op jit(solution)/shard_map/dot_general | solution.py:99
  238.4 10.3 %psum.7 = f32[64,64]{0,1:T(8,128)S(1)} all-reduce(f32[64,64]{0,1:T(8,128)S(1)} %get-tuple-element.244), channel_id=1, replica_groups=mesh['tiles'=8,'chan'=4] {'chan'}, use_global_device_ids=true, to_apply=%region_4.5 | all-reduce | flops 4096 | bytes 32768 | tf_op jit(solution)/shard_map/psum | solution.py:103
  253.0 3.4 %all-to-all-start = ((bf16[8,2,2048]{2,1,0:T(2,128)(2,1)}), bf16[8,2,2048]{2,1,0:T(2,128)(2,1)S(1)}, u32[]{:S(2)}, u32[]{:S(2)}) async-start(bf16[8,2,2048]{2,1,0:T(2,128)(2,1)} %reshape.271), calls=%async_computation | async-start | bytes 131072 | tf_op jit(solution)/shard_map/all_to_all | solution.py:118
  258.7 4.5 %all-to-all-done = bf16[8,2,2048]{2,1,0:T(2,128)(2,1)S(1)} async-done(((bf16[8,2,2048]{2,1,0:T(2,128)(2,1)}), bf16[8,2,2048]{2,1,0:T(2,128)(2,1)S(1)}, u32[]{:S(2)}, u32[]{:S(2)}) %all-to-all-start) | async-done | bytes 65568 | tf_op jit(solution)/shard_map/all_to_all | solution.py:118
  (153 shorter events, 90.4 us)
Async XLA Ops:
  0.6 4.3 %copy-start = (bf16[27,256,64]{1,2,0:T(8,128)(2,1)S(1)}, bf16[27,256,64]{1,2,0:T(8,128)(2,1)}, u32[]{:S(2)}) copy-start(bf16[27,256,64]{1,2,0:T(8,128)(2,1)} %param.10) | copy-start | bytes 2654212
  171.7 19.5 %copy-start.1 = (bf16[64,64,256]{2,1,0:T(8,128)(2,1)S(1)}, bf16[64,64,256]{2,1,0:T(8,128)(2,1)}, u32[]{:S(2)}) copy-start(bf16[64,64,256]{2,1,0:T(8,128)(2,1)} %param.9) | copy-start | bytes 6291460
  174.3 20.4 %collective-permute-start = (bf16[16,64,64]{2,1,0:T(8,128)(2,1)}, bf16[16,64,64]{2,1,0:T(8,128)(2,1)}, u32[]{:S(2)}, u32[]{:S(2)}) collective-permute-start(bf16[16,64,64]{2,1,0:T(8,128)(2,1)} %get-tuple-element.243), channel_id=1, source_target_pairs={{0,4},{4,8},{8,12},{12,16},{16,20},{20,24},{24,28},{1,5},{5,9},{9,... | collective-permute-start | bytes 393224 | tf_op jit(solution)/shard_map/ppermute | solution.py:12
  179.8 17.9 %collective-permute-start.1 = (bf16[16,64,64]{2,1,0:T(8,128)(2,1)}, bf16[16,64,64]{2,1,0:T(8,128)(2,1)}, u32[]{:S(2)}, u32[]{:S(2)}) collective-permute-start(bf16[16,64,64]{2,1,0:T(8,128)(2,1)} %get-tuple-element.242), channel_id=1, source_target_pairs={{0,8},{4,12},{8,16},{12,20},{16,24},{20,28},{1,9},{5,13},{9,17},{1... | collective-permute-start | bytes 393224 | tf_op jit(solution)/shard_map/ppermute | solution.py:12
  183.4 17.3 %collective-permute-start.2 = (bf16[16,64,64]{2,1,0:T(8,128)(2,1)}, bf16[16,64,64]{2,1,0:T(8,128)(2,1)}, u32[]{:S(2)}, u32[]{:S(2)}) collective-permute-start(bf16[16,64,64]{2,1,0:T(8,128)(2,1)} %get-tuple-element.241), channel_id=1, source_target_pairs={{0,12},{4,16},{8,20},{12,24},{16,28},{1,13},{5,17},{9,21},{13,25},... | collective-permute-start | bytes 393224 | tf_op jit(solution)/shard_map/ppermute | solution.py:12
  187.8 16.0 %collective-permute-start.3 = (bf16[16,64,64]{2,1,0:T(8,128)(2,1)S(1)}, bf16[16,64,64]{2,1,0:T(8,128)(2,1)}, u32[]{:S(2)}, u32[]{:S(2)}) collective-permute-start(bf16[16,64,64]{2,1,0:T(8,128)(2,1)S(1)} %get-tuple-element.240), channel_id=1, source_target_pairs={{0,16},{4,20},{8,24},{12,28},{1,17},{5,21},{9,25},{13,29},{2,18},{... | collective-permute-start | bytes 393224 | tf_op jit(solution)/shard_map/ppermute | solution.py:12
  189.8 15.7 %collective-permute-start.4 = (bf16[16,64,64]{2,1,0:T(8,128)(2,1)S(1)}, bf16[16,64,64]{2,1,0:T(8,128)(2,1)}, u32[]{:S(2)}, u32[]{:S(2)}) collective-permute-start(bf16[16,64,64]{2,1,0:T(8,128)(2,1)S(1)} %get-tuple-element.239), channel_id=1, source_target_pairs={{4,0},{8,4},{12,8},{16,12},{20,16},{24,20},{28,24},{5,1},{9,5},{13... | collective-permute-start | bytes 393224 | tf_op jit(solution)/shard_map/ppermute | solution.py:12
  191.1 3.6 %copy-start.5 = (bf16[64]{0:T(256)(128)(2,1)S(1)}, bf16[64]{0:T(256)(128)(2,1)}, u32[]{:S(2)}) copy-start(bf16[64]{0:T(256)(128)(2,1)} %param.11) | copy-start | bytes 388
  194.7 12.4 %collective-permute-start.5 = (bf16[16,64,64]{2,1,0:T(8,128)(2,1)S(1)}, bf16[16,64,64]{2,1,0:T(8,128)(2,1)S(1)}, u32[]{:S(2)}, u32[]{:S(2)}) collective-permute-start(bf16[16,64,64]{2,1,0:T(8,128)(2,1)S(1)} %get-tuple-element.238), channel_id=1, source_target_pairs={{8,0},{12,4},{16,8},{20,12},{24,16},{28,20},{9,1},{13,5},{17,9},{2... | collective-permute-start | bytes 393224 | tf_op jit(solution)/shard_map/ppermute | solution.py:12
  197.7 16.3 %collective-permute-start.6 = (bf16[16,64,64]{2,1,0:T(8,128)(2,1)S(1)}, bf16[16,64,64]{2,1,0:T(8,128)(2,1)S(1)}, u32[]{:S(2)}, u32[]{:S(2)}) collective-permute-start(bf16[16,64,64]{2,1,0:T(8,128)(2,1)S(1)} %get-tuple-element.237), channel_id=1, source_target_pairs={{12,0},{16,4},{20,8},{24,12},{28,16},{13,1},{17,5},{21,9},{25,13},... | collective-permute-start | bytes 393224 | tf_op jit(solution)/shard_map/ppermute | solution.py:12
  200.7 28.6 %collective-permute-start.7 = (bf16[16,64,64]{2,1,0:T(8,128)(2,1)S(1)}, bf16[16,64,64]{2,1,0:T(8,128)(2,1)S(1)}, u32[]{:S(2)}, u32[]{:S(2)}) collective-permute-start(bf16[16,64,64]{2,1,0:T(8,128)(2,1)S(1)} %get-tuple-element.236), channel_id=1, source_target_pairs={{16,0},{20,4},{24,8},{28,12},{17,1},{21,5},{25,9},{29,13},{18,2},{... | collective-permute-start | bytes 393224 | tf_op jit(solution)/shard_map/ppermute | solution.py:12
  230.1 4.6 %copy-start.4 = (s32[1,128]{1,0:T(1,128)S(1)}, s32[1,128]{1,0:T(1,128)}, u32[]{:S(2)}) copy-start(s32[1,128]{1,0:T(1,128)} %param.13) | copy-start | bytes 1540
  251.1 0.8 copy-start.2
  251.3 12.2 %copy-start.3 = (s32[1,8]{1,0:T(1,128)S(1)}, s32[1,8]{1,0:T(1,128)}, u32[]{:S(2)}) copy-start(s32[1,8]{1,0:T(1,128)} %param.15) | copy-start | bytes 100
  253.0 10.2 %all-to-all-start = ((bf16[8,2,2048]{2,1,0:T(2,128)(2,1)}), bf16[8,2,2048]{2,1,0:T(2,128)(2,1)S(1)}, u32[]{:S(2)}, u32[]{:S(2)}) async-start(bf16[8,2,2048]{2,1,0:T(2,128)(2,1)} %reshape.271), calls=%async_computation | async-start | bytes 131072 | tf_op jit(solution)/shard_map/all_to_all | solution.py:118
where the time goes:
time: 266 us; the launch traced here: 265 us
  local copies, waits for them, and re-layouts  101 us (38%)
  matrix products  98.2 us (37%)
  waiting for transfers between devices  25.2 us (9%)
  starting transfers between devices  24.2 us (9%)
  blocking collectives  10.3 us (4%)
  other arithmetic  4.43 us (2%)
    dot_general x6, matrix products, step_rules(): jnp.einsum('bvc,bcq->bvq', chosen, kernels, preferred_element_type=jnp.fl...  43.3 us
    dot_general x6, matrix products, step_rules(): jnp.dot(target_hot, partial_out.reshape(group.shape[0], 64 * quarter), pr...  33.6 us
    dot_general x6, local copies, waits for them, and re-layouts, step_rules(): jnp.einsum('bvc,bcq->bvq', chosen, kernels, preferred_element_type=jnp.fl...  22.7 us
    ppermute x8, starting transfers between devices, from_behind(): return lax.ppermute(block, axis, route)  20.8 us
    ppermute x8, waiting for transfers between devices, from_behind(): return lax.ppermute(block, axis, route)  20.7 us
    unnamed x24, local copies, waits for them, and re-layouts  19.5 us
    while x6, local copies, waits for them, and re-layouts  19.3 us
    dot_general x6, matrix products, step_rules(): jnp.dot(source_hot, flat_features, preferred_element_type=jnp.float32)  17.3 us
  transfers between devices with their start and end apart: 9, of which 3 were waited for; matrix products, arithmetic and copies ran while one was open for 6% of the time, Pallas kernels for 0%

commit v1 on v0

--- a/solution.py
+++ b/solution.py
@@ -100,7 +100,8 @@
         tile_count, 64, quarter
     )
     convolved = totals[:tile_count] + gathered_in
-    squares = lax.psum(jnp.sum(convolved * convolved, axis=-1), "chan")
+    view = jnp.sum(convolved * convolved, axis=-1)
+    squares = lax.all_gather(view, "chan").sum(axis=0)
     mean_square = squares[:, :, None] / channels
     hidden = jax.nn.silu(gain.astype(jnp.float32) * convolved * lax.rsqrt(mean_square + epsilon))
     skip_features = (own_part.astype(jnp.float32) + hidden).astype(jnp.bfloat16)

time: 266 us -> 255 us (0.959)
  local copies, waits for them, and re-layouts: 101 us -> 92.1 us
  blocking collectives: 10.3 us -> 5.42 us
  waiting for transfers between devices: 25.2 us -> 29.9 us
    psum x1 -> x0, blocking collectives: 10.3 us -> none  [body(): squares = lax.psum(jnp.sum(convolved * convolved, axis=-1), 'chan')]
    all_gather x0 -> x1, blocking collectives: none -> 5.42 us  [body(): squares = lax.all_gather(view, 'chan').sum(axis=0)]
    ppermute x8, waiting for transfers between devices: 20.7 us -> 25.4 us  [from_behind(): return lax.ppermute(block, axis, route)]
    unnamed x24, local copies, waits for them, and re-layouts: 19.5 us -> 15.2 us
  transfers between devices with their start and end apart: 9 -> 9, of which waited for: 3 -> 4; matrix products, arithmetic and copies ran while one was open for 6% -> 4% of each run, Pallas kernels for 0% -> 0%
where the time goes in v1:
time: 255 us; the launch traced here: 254 us
  matrix products  96.9 us (38%)
  local copies, waits for them, and re-layouts  92.1 us (36%)
  waiting for transfers between devices  29.9 us (12%)
  starting transfers between devices  24.2 us (9%)
  blocking collectives  5.42 us (2%)
  other arithmetic  4.08 us (2%)
    dot_general x6, matrix products, step_rules(): jnp.einsum('bvc,bcq->bvq', chosen, kernels, preferred_element_type=jnp.fl...  43.3 us
    dot_general x6, matrix products, step_rules(): jnp.dot(target_hot, partial_out.reshape(group.shape[0], 64 * quarter), pr...  33.6 us
    ppermute x8, waiting for transfers between devices, from_behind(): return lax.ppermute(block, axis, route)  25.4 us
    dot_general x6, local copies, waits for them, and re-layouts, step_rules(): jnp.einsum('bvc,bcq->bvq', chosen, kernels, preferred_element_type=jnp.fl...  22.7 us
    ppermute x8, starting transfers between devices, from_behind(): return lax.ppermute(block, axis, route)  20.8 us
    while x6, local copies, waits for them, and re-layouts  19.3 us
    dot_general x6, matrix products, step_rules(): jnp.dot(source_hot, flat_features, preferred_element_type=jnp.float32)  17.3 us
    gather x6, local copies, waits for them, and re-layouts, step_rules(): kernels = weights[jnp.minimum(group[:, 1], 26)]  16.6 us
  transfers between devices with their start and end apart: 9, of which 4 were waited for; matrix products, arithmetic and copies ran while one was open for 4% of the time, Pallas kernels for 0%

profile of v1, /device:TPU:0, one launch (start us, length us, event | category | flops | bytes accessed | tf_op | source)
XLA Modules:
  0.0 254.0 jit_solution(3885448647540461879)
XLA Ops:
  0.7 4.3 %copy.59 = bf16[8,8,64,256]{3,1,2,0:T(8,128)(2,1)} copy(bf16[8,8,64,256]{3,2,1,0:T(8,128)(2,1)} %bitcast.92) | data formatting | bytes 4194304
  4.9 160.6 %while.16 = (s32[]{:T(128)}, f32[192,64,64]{0,2,1:T(8,128)}, s32[6,128,4]{1,2,0:T(4,128)}, bf16[64,16384]{1,0:T(8,128)(2,1)}, bf16[27,256,64]{1,2,0:T(8,128)(2,1)S(1)}, /*index=5*/s32[]{:T(128)}, s32[]{:T(128)}) while((s32[]{:T(128)}, f32[192,64,64]{0,2,1:T(8,128)}, s32[6,128,4]{1,2,0:T(4,128)}, ...), condition=%wide.region_2.3_spmd.clone.clone, body=%wide.region_0.2_spmd.clone.clone.sunk | while | flops 2020381184 | bytes 46548056 | solution.py:91
  9.1 3.2 %copy.64 = bf16[16,8,64,256]{3,2,1,0:T(8,128)(2,1)} copy(bf16[16,8,64,256]{3,1,2,0:T(8,128)(2,1)S(1)} %bitcast.90) | data formatting | bytes 8388608 | tf_op jit(solution)/shard_map/while
  15.1 7.2 %fusion.70 = f32[128,64,64]{2,1,0:T(8,128)} fusion(bf16[128,256,64]{1,2,0:T(8,128)(2,1)} %gather_fusion, bf16[128,64,256]{2,1,0:T(8,128)(2,1)} %bitcast.89, s32[128,64]{1,0:T(8,128)S(1)} %copy.65, pred[128,64]{1,0:T(8,128)(4,1)S(1)} %copy.66), kind=kOutput, calls=%fused_computation.6.clone.1 | convolution fusion | flops 540016640 | bytes 10526720 | tf_op jit(solution)/shard_map/while/body/eval_jaxpr/bvc,bcq->bvq/dot_general | solution.py:78
  22.3 3.8 %copy.67 = f32[128,64,64]{0,2,1:T(8,128)S(1)} copy(f32[128,64,64]{2,1,0:T(8,128)} %fusion.70) | data formatting | bytes 4194304 | tf_op jit(solution)/shard_map/while/body/eval_jaxpr/bvc,bcq->bvq/dot_general | solution.py:78
  26.1 3.8 %select_add_fusion.2 = f32[192,64,64]{0,2,1:T(8,128)} fusion(f32[192,64,64]{0,2,1:T(8,128)} %get-tuple-element.315, f32[128,64,64]{0,2,1:T(8,128)S(1)} %copy.67, pred[]{:T(512)S(6)} %compare.18, s32[128]{0:T(128)S(1)} %get-tuple-element.306), kind=kOutput, calls=%fused_computation.5.clone.1 | convolution fusion | flops 1209556992 | bytes 8389121 | tf_op jit(solution)/shard_map/while/body/eval_jaxpr/dot_general | solution.py:82
  34.0 3.2 %copy.64 = bf16[16,8,64,256]{3,2,1,0:T(8,128)(2,1)} copy(bf16[16,8,64,256]{3,1,2,0:T(8,128)(2,1)S(1)} %bitcast.90) | data formatting | bytes 8388608 | tf_op jit(solution)/shard_map/while
  40.0 7.2 %fusion.70 = f32[128,64,64]{2,1,0:T(8,128)} fusion(bf16[128,256,64]{1,2,0:T(8,128)(2,1)} %gather_fusion, bf16[128,64,256]{2,1,0:T(8,128)(2,1)} %bitcast.89, s32[128,64]{1,0:T(8,128)S(1)} %copy.65, pred[128,64]{1,0:T(8,128)(4,1)S(1)} %copy.66), kind=kOutput, calls=%fused_computation.6.clone.1 | convolution fusion | flops 540016640 | bytes 10526720 | tf_op jit(solution)/shard_map/while/body/eval_jaxpr/bvc,bcq->bvq/dot_general | solution.py:78
  47.2 3.8 %copy.67 = f32[128,64,64]{0,2,1:T(8,128)S(1)} copy(f32[128,64,64]{2,1,0:T(8,128)} %fusion.70) | data formatting | bytes 4194304 | tf_op jit(solution)/shard_map/while/body/eval_jaxpr/bvc,bcq->bvq/dot_general | solution.py:78
  51.0 6.0 %select_add_fusion.2 = f32[192,64,64]{0,2,1:T(8,128)} fusion(f32[192,64,64]{0,2,1:T(8,128)} %get-tuple-element.315, f32[128,64,64]{0,2,1:T(8,128)S(1)} %copy.67, pred[]{:T(512)S(6)} %compare.18, s32[128]{0:T(128)S(1)} %get-tuple-element.306), kind=kOutput, calls=%fused_computation.5.clone.1 | convolution fusion | flops 1209556992 | bytes 8389121 | tf_op jit(solution)/shard_map/while/body/eval_jaxpr/dot_general | solution.py:82
  67.1 7.2 %fusion.70 = f32[128,64,64]{2,1,0:T(8,128)} fusion(bf16[128,256,64]{1,2,0:T(8,128)(2,1)} %gather_fusion, bf16[128,64,256]{2,1,0:T(8,128)(2,1)} %bitcast.89, s32[128,64]{1,0:T(8,128)S(1)} %copy.65, pred[128,64]{1,0:T(8,128)(4,1)S(1)} %copy.66), kind=kOutput, calls=%fused_computation.6.clone.1 | convolution fusion | flops 540016640 | bytes 10526720 | tf_op jit(solution)/shard_map/while/body/eval_jaxpr/bvc,bcq->bvq/dot_general | solution.py:78
  74.4 3.8 %copy.67 = f32[128,64,64]{0,2,1:T(8,128)S(1)} copy(f32[128,64,64]{2,1,0:T(8,128)} %fusion.70) | data formatting | bytes 4194304 | tf_op jit(solution)/shard_map/while/body/eval_jaxpr/bvc,bcq->bvq/dot_general | solution.py:78
  78.2 6.0 %select_add_fusion.2 = f32[192,64,64]{0,2,1:T(8,128)} fusion(f32[192,64,64]{0,2,1:T(8,128)} %get-tuple-element.315, f32[128,64,64]{0,2,1:T(8,128)S(1)} %copy.67, pred[]{:T(512)S(6)} %compare.18, s32[128]{0:T(128)S(1)} %get-tuple-element.306), kind=kOutput, calls=%fused_computation.5.clone.1 | convolution fusion | flops 1209556992 | bytes 8389121 | tf_op jit(solution)/shard_map/while/body/eval_jaxpr/dot_general | solution.py:82
  88.3 3.2 %copy.64 = bf16[16,8,64,256]{3,2,1,0:T(8,128)(2,1)} copy(bf16[16,8,64,256]{3,1,2,0:T(8,128)(2,1)S(1)} %bitcast.90) | data formatting | bytes 8388608 | tf_op jit(solution)/shard_map/while
  94.3 7.2 %fusion.70 = f32[128,64,64]{2,1,0:T(8,128)} fusion(bf16[128,256,64]{1,2,0:T(8,128)(2,1)} %gather_fusion, bf16[128,64,256]{2,1,0:T(8,128)(2,1)} %bitcast.89, s32[128,64]{1,0:T(8,128)S(1)} %copy.65, pred[128,64]{1,0:T(8,128)(4,1)S(1)} %copy.66), kind=kOutput, calls=%fused_computation.6.clone.1 | convolution fusion | flops 540016640 | bytes 10526720 | tf_op jit(solution)/shard_map/while/body/eval_jaxpr/bvc,bcq->bvq/dot_general | solution.py:78
  101.5 3.8 %copy.67 = f32[128,64,64]{0,2,1:T(8,128)S(1)} copy(f32[128,64,64]{2,1,0:T(8,128)} %fusion.70) | data formatting | bytes 4194304 | tf_op jit(solution)/shard_map/while/body/eval_jaxpr/bvc,bcq->bvq/dot_general | solution.py:78
  105.3 6.0 %select_add_fusion.2 = f32[192,64,64]{0,2,1:T(8,128)} fusion(f32[192,64,64]{0,2,1:T(8,128)} %get-tuple-element.315, f32[128,64,64]{0,2,1:T(8,128)S(1)} %copy.67, pred[]{:T(512)S(6)} %compare.18, s32[128]{0:T(128)S(1)} %get-tuple-element.306), kind=kOutput, calls=%fused_computation.5.clone.1 | convolution fusion | flops 1209556992 | bytes 8389121 | tf_op jit(solution)/shard_map/while/body/eval_jaxpr/dot_general | solution.py:82
  121.4 7.2 %fusion.70 = f32[128,64,64]{2,1,0:T(8,128)} fusion(bf16[128,256,64]{1,2,0:T(8,128)(2,1)} %gather_fusion, bf16[128,64,256]{2,1,0:T(8,128)(2,1)} %bitcast.89, s32[128,64]{1,0:T(8,128)S(1)} %copy.65, pred[128,64]{1,0:T(8,128)(4,1)S(1)} %copy.66), kind=kOutput, calls=%fused_computation.6.clone.1 | convolution fusion | flops 540016640 | bytes 10526720 | tf_op jit(solution)/shard_map/while/body/eval_jaxpr/bvc,bcq->bvq/dot_general | solution.py:78
  128.6 3.8 %copy.67 = f32[128,64,64]{0,2,1:T(8,128)S(1)} copy(f32[128,64,64]{2,1,0:T(8,128)} %fusion.70) | data formatting | bytes 4194304 | tf_op jit(solution)/shard_map/while/body/eval_jaxpr/bvc,bcq->bvq/dot_general | solution.py:78
  132.4 6.0 %select_add_fusion.2 = f32[192,64,64]{0,2,1:T(8,128)} fusion(f32[192,64,64]{0,2,1:T(8,128)} %get-tuple-element.315, f32[128,64,64]{0,2,1:T(8,128)S(1)} %copy.67, pred[]{:T(512)S(6)} %compare.18, s32[128]{0:T(128)S(1)} %get-tuple-element.306), kind=kOutput, calls=%fused_computation.5.clone.1 | convolution fusion | flops 1209556992 | bytes 8389121 | tf_op jit(solution)/shard_map/while/body/eval_jaxpr/dot_general | solution.py:82
  148.5 7.2 %fusion.70 = f32[128,64,64]{2,1,0:T(8,128)} fusion(bf16[128,256,64]{1,2,0:T(8,128)(2,1)} %gather_fusion, bf16[128,64,256]{2,1,0:T(8,128)(2,1)} %bitcast.89, s32[128,64]{1,0:T(8,128)S(1)} %copy.65, pred[128,64]{1,0:T(8,128)(4,1)S(1)} %copy.66), kind=kOutput, calls=%fused_computation.6.clone.1 | convolution fusion | flops 540016640 | bytes 10526720 | tf_op jit(solution)/shard_map/while/body/eval_jaxpr/bvc,bcq->bvq/dot_general | solution.py:78
  155.7 3.8 %copy.67 = f32[128,64,64]{0,2,1:T(8,128)S(1)} copy(f32[128,64,64]{2,1,0:T(8,128)} %fusion.70) | data formatting | bytes 4194304 | tf_op jit(solution)/shard_map/while/body/eval_jaxpr/bvc,bcq->bvq/dot_general | solution.py:78
  159.5 6.0 %select_add_fusion.2 = f32[192,64,64]{0,2,1:T(8,128)} fusion(f32[192,64,64]{0,2,1:T(8,128)} %get-tuple-element.315, f32[128,64,64]{0,2,1:T(8,128)S(1)} %copy.67, pred[]{:T(512)S(6)} %compare.18, s32[128]{0:T(128)S(1)} %get-tuple-element.306), kind=kOutput, calls=%fused_computation.5.clone.1 | convolution fusion | flops 1209556992 | bytes 8389121 | tf_op jit(solution)/shard_map/while/body/eval_jaxpr/dot_general | solution.py:82
  165.5 5.2 %copy.50 = bf16[192,64,64]{2,1,0:T(8,128)(2,1)S(1)} copy(f32[192,64,64]{0,2,1:T(8,128)} %get-tuple-element.164) | data formatting | bytes 4718592 | tf_op jit(solution)/shard_map/while | solution.py:91
  171.9 4.8 %collective-permute-start = (bf16[16,64,64]{2,1,0:T(8,128)(2,1)}, bf16[16,64,64]{2,1,0:T(8,128)(2,1)S(1)}, u32[]{:S(2)}, u32[]{:S(2)}) collective-permute-start(bf16[16,64,64]{2,1,0:T(8,128)(2,1)} %get-tuple-element.247), channel_id=1, source_target_pairs={{0,4},{4,8},{8,12},{12,16},{16,20},{20,24},{24,28},{1,5},{5,9},{9,... | collective-permute-start | bytes 393224 | tf_op jit(solution)/shard_map/ppermute | solution.py:12
  176.8 4.2 %collective-permute-start.1 = (bf16[16,64,64]{2,1,0:T(8,128)(2,1)}, bf16[16,64,64]{2,1,0:T(8,128)(2,1)}, u32[]{:S(2)}, u32[]{:S(2)}) collective-permute-start(bf16[16,64,64]{2,1,0:T(8,128)(2,1)} %get-tuple-element.246), channel_id=1, source_target_pairs={{0,8},{4,12},{8,16},{12,20},{16,24},{20,28},{1,9},{5,13},{9,17},{1... | collective-permute-start | bytes 393224 | tf_op jit(solution)/shard_map/ppermute | solution.py:12
  181.0 4.5 %collective-permute-start.2 = (bf16[16,64,64]{2,1,0:T(8,128)(2,1)}, bf16[16,64,64]{2,1,0:T(8,128)(2,1)}, u32[]{:S(2)}, u32[]{:S(2)}) collective-permute-start(bf16[16,64,64]{2,1,0:T(8,128)(2,1)} %get-tuple-element.245), channel_id=1, source_target_pairs={{0,12},{4,16},{8,20},{12,24},{16,28},{1,13},{5,17},{9,21},{13,25},... | collective-permute-start | bytes 393224 | tf_op jit(solution)/shard_map/ppermute | solution.py:12
  204.3 8.2 %collective-permute-done.6 = bf16[16,64,64]{2,1,0:T(8,128)(2,1)S(1)} collective-permute-done((bf16[16,64,64]{2,1,0:T(8,128)(2,1)}, bf16[16,64,64]{2,1,0:T(8,128)(2,1)S(1)}, u32[]{:S(2)}, u32[]{:S(2)}) %collective-permute-start.6) | collective-permute-done | bytes 131104 | tf_op jit(solution)/shard_map/ppermute | solution.py:12
  212.6 14.9 %collective-permute-done.7 = bf16[16,64,64]{2,1,0:T(8,128)(2,1)S(1)} collective-permute-done((bf16[16,64,64]{2,1,0:T(8,128)(2,1)S(1)}, bf16[16,64,64]{2,1,0:T(8,128)(2,1)S(1)}, u32[]{:S(2)}, u32[]{:S(2)}) %collective-permute-start.7) | collective-permute-done | bytes 131104 | tf_op jit(solution)/shard_map/ppermute | solution.py:12
  233.0 5.4 %all-gather = f32[256,64]{1,0:T(8,128)S(1)} all-gather(f32[64,64]{1,0:T(8,128)S(1)} %copy.52), channel_id=2, replica_groups=mesh['tiles'=8,'chan'=4] {'chan'}, dimensions={0}, use_global_device_ids=true | all-gather | bytes 81920 | tf_op jit(solution)/shard_map/all_gather | solution.py:104
  242.5 3.4 %all-to-all-start = ((bf16[8,2,2048]{2,1,0:T(2,128)(2,1)}), bf16[8,2,2048]{2,1,0:T(2,128)(2,1)S(1)}, u32[]{:S(2)}, u32[]{:S(2)}) async-start(bf16[8,2,2048]{2,1,0:T(2,128)(2,1)} %reshape.276), calls=%async_computation | async-start | bytes 131072 | tf_op jit(solution)/shard_map/all_to_all | solution.py:119
  248.2 4.5 %all-to-all-done = bf16[8,2,2048]{2,1,0:T(2,128)(2,1)S(1)} async-done(((bf16[8,2,2048]{2,1,0:T(2,128)(2,1)}), bf16[8,2,2048]{2,1,0:T(2,128)(2,1)S(1)}, u32[]{:S(2)}, u32[]{:S(2)}) %all-to-all-start) | async-done | bytes 65568 | tf_op jit(solution)/shard_map/all_to_all | solution.py:119
  (156 shorter events, 83.9 us)
Async XLA Ops:
  0.6 4.3 %copy-start = (bf16[27,256,64]{1,2,0:T(8,128)(2,1)S(1)}, bf16[27,256,64]{1,2,0:T(8,128)(2,1)}, u32[]{:S(2)}) copy-start(bf16[27,256,64]{1,2,0:T(8,128)(2,1)} %param.10) | copy-start | bytes 2654212
  171.9 20.4 %collective-permute-start = (bf16[16,64,64]{2,1,0:T(8,128)(2,1)}, bf16[16,64,64]{2,1,0:T(8,128)(2,1)S(1)}, u32[]{:S(2)}, u32[]{:S(2)}) collective-permute-start(bf16[16,64,64]{2,1,0:T(8,128)(2,1)} %get-tuple-element.247), channel_id=1, source_target_pairs={{0,4},{4,8},{8,12},{12,16},{16,20},{20,24},{24,28},{1,5},{5,9},{9,... | collective-permute-start | bytes 393224 | tf_op jit(solution)/shard_map/ppermute | solution.py:12
  176.8 18.5 %collective-permute-start.1 = (bf16[16,64,64]{2,1,0:T(8,128)(2,1)}, bf16[16,64,64]{2,1,0:T(8,128)(2,1)}, u32[]{:S(2)}, u32[]{:S(2)}) collective-permute-start(bf16[16,64,64]{2,1,0:T(8,128)(2,1)} %get-tuple-element.246), channel_id=1, source_target_pairs={{0,8},{4,12},{8,16},{12,20},{16,24},{20,28},{1,9},{5,13},{9,17},{1... | collective-permute-start | bytes 393224 | tf_op jit(solution)/shard_map/ppermute | solution.py:12
  181.0 16.6 %collective-permute-start.2 = (bf16[16,64,64]{2,1,0:T(8,128)(2,1)}, bf16[16,64,64]{2,1,0:T(8,128)(2,1)}, u32[]{:S(2)}, u32[]{:S(2)}) collective-permute-start(bf16[16,64,64]{2,1,0:T(8,128)(2,1)} %get-tuple-element.245), channel_id=1, source_target_pairs={{0,12},{4,16},{8,20},{12,24},{16,28},{1,13},{5,17},{9,21},{13,25},... | collective-permute-start | bytes 393224 | tf_op jit(solution)/shard_map/ppermute | solution.py:12
  185.4 14.6 %collective-permute-start.3 = (bf16[16,64,64]{2,1,0:T(8,128)(2,1)}, bf16[16,64,64]{2,1,0:T(8,128)(2,1)}, u32[]{:S(2)}, u32[]{:S(2)}) collective-permute-start(bf16[16,64,64]{2,1,0:T(8,128)(2,1)} %get-tuple-element.244), channel_id=1, source_target_pairs={{0,16},{4,20},{8,24},{12,28},{1,17},{5,21},{9,25},{13,29},{2,18},{... | collective-permute-start | bytes 393224 | tf_op jit(solution)/shard_map/ppermute | solution.py:12
  187.4 13.6 %collective-permute-start.4 = (bf16[16,64,64]{2,1,0:T(8,128)(2,1)}, bf16[16,64,64]{2,1,0:T(8,128)(2,1)}, u32[]{:S(2)}, u32[]{:S(2)}) collective-permute-start(bf16[16,64,64]{2,1,0:T(8,128)(2,1)} %get-tuple-element.243), channel_id=1, source_target_pairs={{4,0},{8,4},{12,8},{16,12},{20,16},{24,20},{28,24},{5,1},{9,5},{13... | collective-permute-start | bytes 393224 | tf_op jit(solution)/shard_map/ppermute | solution.py:12
  188.7 3.6 %copy-start.5 = (bf16[64]{0:T(256)(128)(2,1)S(1)}, bf16[64]{0:T(256)(128)(2,1)}, u32[]{:S(2)}) copy-start(bf16[64]{0:T(256)(128)(2,1)} %param.11) | copy-start | bytes 388
  192.3 0.7 copy-start.1
  193.0 11.3 %collective-permute-start.5 = (bf16[16,64,64]{2,1,0:T(8,128)(2,1)}, bf16[16,64,64]{2,1,0:T(8,128)(2,1)S(1)}, u32[]{:S(2)}, u32[]{:S(2)}) collective-permute-start(bf16[16,64,64]{2,1,0:T(8,128)(2,1)} %get-tuple-element.242), channel_id=1, source_target_pairs={{8,0},{12,4},{16,8},{20,12},{24,16},{28,20},{9,1},{13,5},{17,9},{2... | collective-permute-start | bytes 393224 | tf_op jit(solution)/shard_map/ppermute | solution.py:12
  195.3 17.3 %collective-permute-start.6 = (bf16[16,64,64]{2,1,0:T(8,128)(2,1)}, bf16[16,64,64]{2,1,0:T(8,128)(2,1)S(1)}, u32[]{:S(2)}, u32[]{:S(2)}) collective-permute-start(bf16[16,64,64]{2,1,0:T(8,128)(2,1)} %get-tuple-element.241), channel_id=1, source_target_pairs={{12,0},{16,4},{20,8},{24,12},{28,16},{13,1},{17,5},{21,9},{25,13},... | collective-permute-start | bytes 393224 | tf_op jit(solution)/shard_map/ppermute | solution.py:12
  197.6 29.9 %collective-permute-start.7 = (bf16[16,64,64]{2,1,0:T(8,128)(2,1)S(1)}, bf16[16,64,64]{2,1,0:T(8,128)(2,1)S(1)}, u32[]{:S(2)}, u32[]{:S(2)}) collective-permute-start(bf16[16,64,64]{2,1,0:T(8,128)(2,1)S(1)} %get-tuple-element.240), channel_id=1, source_target_pairs={{16,0},{20,4},{24,8},{28,12},{17,1},{21,5},{25,9},{29,13},{18,2},{... | collective-permute-start | bytes 393224 | tf_op jit(solution)/shard_map/ppermute | solution.py:12
  227.5 3.0 %copy-start.4 = (s32[1,128]{1,0:T(1,128)S(1)}, s32[1,128]{1,0:T(1,128)}, u32[]{:S(2)}) copy-start(s32[1,128]{1,0:T(1,128)} %param.13) | copy-start | bytes 1540
  240.6 0.8 copy-start.2
  240.8 12.2 %copy-start.3 = (s32[1,8]{1,0:T(1,128)S(1)}, s32[1,8]{1,0:T(1,128)}, u32[]{:S(2)}) copy-start(s32[1,8]{1,0:T(1,128)} %param.15) | copy-start | bytes 100
  242.5 10.2 %all-to-all-start = ((bf16[8,2,2048]{2,1,0:T(2,128)(2,1)}), bf16[8,2,2048]{2,1,0:T(2,128)(2,1)S(1)}, u32[]{:S(2)}, u32[]{:S(2)}) async-start(bf16[8,2,2048]{2,1,0:T(2,128)(2,1)} %reshape.276), calls=%async_computation | async-start | bytes 131072 | tf_op jit(solution)/shard_map/all_to_all | solution.py:119
